TPU v7x, 512 devices: a whole 4x8x8 slice. The times are simulated.
512 devices in a mesh: ch: 128 (over y, z, core), grp: 4 (over x).
Axes of the slice: x: 4, y: 8, z: 8, core: 2. Of those that a mesh axis runs over, the one named last changes fastest.
Arguments:
- raw: bfloat16 [4, 1024, 2048], P('grp', 'ch'), may hold values from -400 to 400
- order: int32 [128, 16], P('ch'), may hold values from 0 to 15, each once within a row
- pair_blocks: int32 [128, 3], P('ch'), may hold values from -1 to 15, as said below
Outputs:
- corr: bfloat16 [2048, 3, 128, 256], P(('ch', 'grp'))
Inputs may be any that keep to these rules, and one draw needn't show every extreme that they name: `pair_blocks`: row i names distinct blocks among i * 16 // 128 - 1, i * 16 // 128, i * 16 // 128 + 1 that lie in 0 .. 15; slot 0 is always i * 16 // 128; live slots come first and empty ones hold -1.
All inputs are finite; a program needn't handle non-finite values.
Results may differ from a plain program's by a relative error of at most 0.013.
Values may be sent and summed in bfloat16 or wider, within the bound.
A program may use at most 128 MiB of HBM per device.

v0:
```python
import math
import jax
import jax.numpy as jnp
from jax import lax
from jax.sharding import PartitionSpec as P

SRC = 128
SEG = 256
LAGS = 256
SMOOTH = 8
MAXP = 3
REACH = 15
lag_scale = 1.0 / 16.0


def from_behind(value, axis, steps):
    count = lax.axis_size(axis)
    initial, last = (max(0, -steps), min(count, count - steps))
    return lax.ppermute(value, axis, [(source, source + steps) for source in range(initial, last)])


def transform_tables(half_len, lag_count, smooth_half):
    samples = jnp.arange(half_len, dtype=jnp.int32)
    column = jnp.arange(2 * half_len, dtype=jnp.int32)
    freq = column % half_len + 1
    phase_fwd = samples[:, None] * freq[None, :] % (2 * half_len)
    angle_fwd = phase_fwd.astype(jnp.float32) * (math.pi / half_len)
    forward = jnp.where(column[None, :] < half_len, jnp.cos(angle_fwd), -jnp.sin(angle_fwd)).astype(
        jnp.bfloat16
    )
    lag_steps = jnp.arange(lag_count, dtype=jnp.int32) - lag_count // 2
    phase_inv = freq[:, None] * lag_steps[None, :] % (2 * half_len)
    angle_inv = phase_inv.astype(jnp.float32) * (math.pi / half_len)
    inverse = (
        jnp.where(column[:, None] < half_len, jnp.cos(angle_inv), -jnp.sin(angle_inv)) * lag_scale
    ).astype(jnp.bfloat16)
    bins = jnp.arange(half_len, dtype=jnp.int32)
    smoothing = (jnp.abs(bins[:, None] - bins[None, :]) <= smooth_half).astype(jnp.float32) / (
        2 * smooth_half + 1
    )
    return (forward, inverse, smoothing)


def whiten(segments, forward, smoothing):
    half_len = segments.shape[-1]
    flat_rows = segments.reshape(-1, half_len)
    spectrum = jnp.dot(flat_rows, forward, preferred_element_type=jnp.float32)
    real_part = spectrum[:, :half_len]
    imag_part = spectrum[:, half_len:]
    power_bins = real_part * real_part + imag_part * imag_part
    smoothed = jnp.dot(power_bins, smoothing, precision=lax.Precision.HIGHEST)
    water_level = jnp.mean(power_bins, axis=1, keepdims=True)
    divisor = jnp.sqrt(smoothed + 0.1 * water_level + 1e-06)
    whitened = spectrum / jnp.concatenate([divisor, divisor], axis=1)
    return whitened.astype(jnp.bfloat16).reshape(segments.shape[:-1] + (2 * half_len,))


def correlate(receivers, sources, inverse):
    half_len = receivers.shape[-1] // 2
    seg_count = receivers.shape[1]
    recv_re = receivers[..., :half_len]
    recv_im = receivers[..., half_len:]
    left_first = jnp.concatenate([recv_re, recv_im], axis=1)
    left_second = jnp.concatenate([recv_im, -recv_re], axis=1)
    right_both = jnp.concatenate([sources[..., :half_len], sources[..., half_len:]], axis=1)
    cross_re = jnp.einsum(
        "rnk,snk->rsk", left_first, right_both, preferred_element_type=jnp.float32
    )
    cross_im = jnp.einsum(
        "rnk,snk->rsk", left_second, right_both, preferred_element_type=jnp.float32
    )
    cross_spec = (jnp.concatenate([cross_re, cross_im], axis=2) * (1.0 / seg_count)).astype(
        jnp.bfloat16
    )
    recv_count = receivers.shape[0]
    src_count = sources.shape[0]
    lag_values = jnp.dot(
        cross_spec.reshape(-1, 2 * half_len), inverse, preferred_element_type=jnp.float32
    )
    return lag_values.reshape(recv_count, src_count, inverse.shape[1])


def local(raw, order, pair_blocks):
    recorded = lax.all_to_all(raw, "ch", split_axis=2, concat_axis=1, tiled=True)
    local_channels = recorded.shape[2]
    onehot = (order[0][:, None] == jnp.arange(local_channels, dtype=jnp.int32)[None, :]).astype(
        jnp.bfloat16
    )
    series = jnp.einsum(
        "ck,tc->kt", onehot, recorded[0], preferred_element_type=jnp.float32
    ).astype(jnp.bfloat16)
    segments = series.reshape(1, local_channels, -1, SEG)
    forward, inverse, smoothing = transform_tables(SEG, LAGS, SMOOTH)
    own_white = whiten(segments, forward, smoothing)
    before_list = []
    for distance in range(REACH, 0, -1):
        before_list.append(from_behind(own_white, "ch", distance))
    after_list = []
    for distance in range(1, REACH + 1):
        after_list.append(from_behind(own_white, "ch", -distance))
    window = jnp.concatenate(before_list + [own_white] + after_list, axis=1)
    window_base = (lax.axis_index("ch") - REACH) * local_channels
    groups = lax.axis_size("grp")
    receivers = own_white[0]
    slot_results = []
    for slot_index in range(MAXP):
        block_id = pair_blocks[0, slot_index]
        source_start = jnp.maximum(block_id, 0) * SRC - window_base
        sources = lax.dynamic_slice_in_dim(window[0], source_start, SRC, 0)
        is_live = (block_id >= 0).astype(jnp.float32)
        lag_values = correlate(receivers, sources, inverse) * is_live
        slot_results.append(lag_values)
    stacked = lax.psum_scatter(
        jnp.stack(slot_results, axis=1).astype(jnp.bfloat16), "grp", scatter_dimension=0, tiled=True
    ).astype(jnp.float32)
    return (stacked / groups).astype(jnp.bfloat16)


def solution(mesh):
    placed = (P("grp", "ch", None), P("ch", None), P("ch", None))
    return jax.shard_map(
        local,
        mesh=mesh,
        in_specs=placed,
        out_specs=P(("ch", "grp"), None, None, None),
        check_vma=False,
    )
```

profile of v0, /device:TPU:1, one launch (start us, length us, event | category | flops | bytes accessed | tf_op | source)
XLA Modules:
  0.0 307.8 jit_solution(12834081129532482578)
XLA Ops:
  6.5 3.1 %copy.19 = bf16[1,8,2048]{1,0,2:T(2,128)(2,1)} copy(bf16[1,8,2048]{2,1,0:T(8,128)(2,1)} %param.3) | data formatting | bytes 65536 | tf_op args[0]
  9.7 18.5 %all-to-all-start = ((bf16[1,8,2048]{1,0,2:T(2,128)(2,1)}), bf16[1,8,2048]{1,0,2:T(2,128)(2,1)S(1)}, u32[]{:S(2)}, u32[]{:S(2)}) async-start(bf16[1,8,2048]{1,0,2:T(2,128)(2,1)} %copy.19), calls=%async_computation | async-start | bytes 2097152 | tf_op jit(solution)/shard_map/all_to_all | solution.py:84
  28.3 0.6 fusion.99
  32.8 25.9 %all-to-all-done = bf16[1,8,2048]{1,0,2:T(2,128)(2,1)S(1)} async-done(((bf16[1,8,2048]{1,0,2:T(2,128)(2,1)}), bf16[1,8,2048]{1,0,2:T(2,128)(2,1)S(1)}, u32[]{:S(2)}, u32[]{:S(2)}) %all-to-all-start) | async-done | bytes 32800 | tf_op jit(solution)/shard_map/all_to_all | solution.py:84
  59.7 2.4 fusion.48
  62.6 4.5 %collective-permute-start = (bf16[1,16,4,512]{3,2,1,0:T(4,128)(2,1)S(1)}, bf16[1,16,4,512]{3,2,1,0:T(4,128)(2,1)S(1)}, u32[]{:S(2)}, u32[]{:S(2)}) collective-permute-start(bf16[1,16,4,512]{3,2,1,0:T(4,128)(2,1)S(1)} %reshape.97), channel_id=1, source_target_pairs={{0,60},{4,64},{8,68},{12,72},{16,76},{20,80},{24,84},{28,88},{32,9... | collective-permute-start | bytes 196616 | tf_op jit(solution)/shard_map/ppermute | solution.py:19
  67.1 1.4 collective-permute-start.1
  68.4 3.3 %collective-permute-start.2 = (bf16[1,16,4,512]{3,2,1,0:T(4,128)(2,1)S(1)}, bf16[1,16,4,512]{3,2,1,0:T(4,128)(2,1)S(1)}, u32[]{:S(2)}, u32[]{:S(2)}) collective-permute-start(bf16[1,16,4,512]{3,2,1,0:T(4,128)(2,1)S(1)} %reshape.97), channel_id=1, source_target_pairs={{0,52},{4,56},{8,60},{12,64},{16,68},{20,72},{24,76},{28,80},{32,8... | collective-permute-start | bytes 196616 | tf_op jit(solution)/shard_map/ppermute | solution.py:19
  71.7 4.7 %collective-permute-start.3 = (bf16[1,16,4,512]{3,2,1,0:T(4,128)(2,1)S(1)}, bf16[1,16,4,512]{3,2,1,0:T(4,128)(2,1)S(1)}, u32[]{:S(2)}, u32[]{:S(2)}) collective-permute-start(bf16[1,16,4,512]{3,2,1,0:T(4,128)(2,1)S(1)} %reshape.97), channel_id=1, source_target_pairs={{0,48},{4,52},{8,56},{12,60},{16,64},{20,68},{24,72},{28,76},{32,8... | collective-permute-start | bytes 196616 | tf_op jit(solution)/shard_map/ppermute | solution.py:19
  76.5 4.3 %collective-permute-start.4 = (bf16[1,16,4,512]{3,2,1,0:T(4,128)(2,1)S(1)}, bf16[1,16,4,512]{3,2,1,0:T(4,128)(2,1)S(1)}, u32[]{:S(2)}, u32[]{:S(2)}) collective-permute-start(bf16[1,16,4,512]{3,2,1,0:T(4,128)(2,1)S(1)} %reshape.97), channel_id=1, source_target_pairs={{0,44},{4,48},{8,52},{12,56},{16,60},{20,64},{24,68},{28,72},{32,7... | collective-permute-start | bytes 196616 | tf_op jit(solution)/shard_map/ppermute | solution.py:19
  81.6 3.6 %collective-permute-start.5 = (bf16[1,16,4,512]{3,2,1,0:T(4,128)(2,1)S(1)}, bf16[1,16,4,512]{3,2,1,0:T(4,128)(2,1)S(1)}, u32[]{:S(2)}, u32[]{:S(2)}) collective-permute-start(bf16[1,16,4,512]{3,2,1,0:T(4,128)(2,1)S(1)} %reshape.97), channel_id=1, source_target_pairs={{0,40},{4,44},{8,48},{12,52},{16,56},{20,60},{24,64},{28,68},{32,7... | collective-permute-start | bytes 196616 | tf_op jit(solution)/shard_map/ppermute | solution.py:19
  85.3 5.7 %collective-permute-start.6 = (bf16[1,16,4,512]{3,2,1,0:T(4,128)(2,1)S(1)}, bf16[1,16,4,512]{3,2,1,0:T(4,128)(2,1)S(1)}, u32[]{:S(2)}, u32[]{:S(2)}) collective-permute-start(bf16[1,16,4,512]{3,2,1,0:T(4,128)(2,1)S(1)} %reshape.97), channel_id=1, source_target_pairs={{0,36},{4,40},{8,44},{12,48},{16,52},{20,56},{24,60},{28,64},{32,6... | collective-permute-start | bytes 196616 | tf_op jit(solution)/shard_map/ppermute | solution.py:19
  91.1 3.6 %collective-permute-start.7 = (bf16[1,16,4,512]{3,2,1,0:T(4,128)(2,1)S(1)}, bf16[1,16,4,512]{3,2,1,0:T(4,128)(2,1)S(1)}, u32[]{:S(2)}, u32[]{:S(2)}) collective-permute-start(bf16[1,16,4,512]{3,2,1,0:T(4,128)(2,1)S(1)} %reshape.97), channel_id=1, source_target_pairs={{0,32},{4,36},{8,40},{12,44},{16,48},{20,52},{24,56},{28,60},{32,6... | collective-permute-start | bytes 196616 | tf_op jit(solution)/shard_map/ppermute | solution.py:19
  94.8 7.2 %collective-permute-start.8 = (bf16[1,16,4,512]{3,2,1,0:T(4,128)(2,1)S(1)}, bf16[1,16,4,512]{3,2,1,0:T(4,128)(2,1)S(1)}, u32[]{:S(2)}, u32[]{:S(2)}) collective-permute-start(bf16[1,16,4,512]{3,2,1,0:T(4,128)(2,1)S(1)} %reshape.97), channel_id=1, source_target_pairs={{0,28},{4,32},{8,36},{12,40},{16,44},{20,48},{24,52},{28,56},{32,6... | collective-permute-start | bytes 196616 | tf_op jit(solution)/shard_map/ppermute | solution.py:19
  102.0 1.3 collective-permute-start.9
  103.3 4.9 %collective-permute-start.10 = (bf16[1,16,4,512]{3,2,1,0:T(4,128)(2,1)S(1)}, bf16[1,16,4,512]{3,2,1,0:T(4,128)(2,1)S(1)}, u32[]{:S(2)}, u32[]{:S(2)}) collective-permute-start(bf16[1,16,4,512]{3,2,1,0:T(4,128)(2,1)S(1)} %reshape.97), channel_id=1, source_target_pairs={{0,20},{4,24},{8,28},{12,32},{16,36},{20,40},{24,44},{28,48},{32,5... | collective-permute-start | bytes 196616 | tf_op jit(solution)/shard_map/ppermute | solution.py:19
  108.3 4.0 %collective-permute-start.11 = (bf16[1,16,4,512]{3,2,1,0:T(4,128)(2,1)S(1)}, bf16[1,16,4,512]{3,2,1,0:T(4,128)(2,1)S(1)}, u32[]{:S(2)}, u32[]{:S(2)}) collective-permute-start(bf16[1,16,4,512]{3,2,1,0:T(4,128)(2,1)S(1)} %reshape.97), channel_id=1, source_target_pairs={{0,16},{4,20},{8,24},{12,28},{16,32},{20,36},{24,40},{28,44},{32,4... | collective-permute-start | bytes 196616 | tf_op jit(solution)/shard_map/ppermute | solution.py:19
  112.4 5.1 %collective-permute-start.12 = (bf16[1,16,4,512]{3,2,1,0:T(4,128)(2,1)S(1)}, bf16[1,16,4,512]{3,2,1,0:T(4,128)(2,1)S(1)}, u32[]{:S(2)}, u32[]{:S(2)}) collective-permute-start(bf16[1,16,4,512]{3,2,1,0:T(4,128)(2,1)S(1)} %reshape.97), channel_id=1, source_target_pairs={{0,12},{4,16},{8,20},{12,24},{16,28},{20,32},{24,36},{28,40},{32,4... | collective-permute-start | bytes 196616 | tf_op jit(solution)/shard_map/ppermute | solution.py:19
  117.5 1.7 collective-permute-start.13
  119.3 2.7 collective-permute-start.14
  122.0 1.9 collective-permute-start.15
  124.0 1.3 collective-permute-start.16
  125.3 1.3 collective-permute-start.17
  126.7 1.3 collective-permute-start.18
  128.0 1.3 collective-permute-start.19
  129.4 1.3 collective-permute-start.20
  130.8 1.3 collective-permute-start.21
  132.1 1.5 collective-permute-done.17
  133.6 1.3 collective-permute-start.22
  134.9 0.7 collective-permute-done.18
  135.6 1.3 collective-permute-start.23
  136.9 2.9 collective-permute-done.19
  139.8 1.3 collective-permute-start.24
  141.1 2.4 collective-permute-done.20
  143.5 1.3 collective-permute-start.25
  144.8 1.3 collective-permute-start.26
  146.3 1.3 collective-permute-start.27
  147.6 1.1 collective-permute-done.23
  148.7 1.3 collective-permute-start.28
  150.0 1.4 collective-permute-done.24
  151.4 1.3 collective-permute-start.29
  152.7 4.3 %collective-permute-done.25 = bf16[1,16,4,512]{3,2,1,0:T(4,128)(2,1)S(1)} collective-permute-done((bf16[1,16,4,512]{3,2,1,0:T(4,128)(2,1)S(1)}, bf16[1,16,4,512]{3,2,1,0:T(4,128)(2,1)S(1)}, u32[]{:S(2)}, u32[]{:S(2)}) %collective-permute-start.25) | collective-permute-done | bytes 65568 | tf_op jit(solution)/shard_map/ppermute | solution.py:19
  157.0 2.7 collective-permute-done.26
  159.7 8.3 %collective-permute-done.27 = bf16[1,16,4,512]{3,2,1,0:T(4,128)(2,1)S(1)} collective-permute-done((bf16[1,16,4,512]{3,2,1,0:T(4,128)(2,1)S(1)}, bf16[1,16,4,512]{3,2,1,0:T(4,128)(2,1)S(1)}, u32[]{:S(2)}, u32[]{:S(2)}) %collective-permute-start.27) | collective-permute-done | bytes 65568 | tf_op jit(solution)/shard_map/ppermute | solution.py:19
  168.6 2.2 collective-permute-done.29
  170.7 1.5 constant_dynamic-slice_fusion.2
  173.6 1.9 convolution_bitcast_fusion.4
  175.6 2.1 copy.26
  177.7 1.2 fusion.96
  178.9 2.0 convolution_bitcast_fusion.3
  180.9 1.9 convolution_bitcast_fusion.2
  182.8 2.2 copy.30
  185.0 1.2 fusion.97
  187.4 1.0 copy-done
  188.8 1.2 copy-done.1
  190.0 0.6 copy-done.2
  191.0 3.4 %fusion.15 = bf16[16,1,128,256]{3,2,0,1:T(8,128)(2,1)S(1)} fusion(bf16[16,128,512]{1,0,2:T(8,128)(2,1)S(1)} %fusion, f32[]{:T(128)} %bitcast.8, s32[256]{0:T(256)S(1)} %iota_add_fusion, s32[512]{0:T(512)S(1)} %fusion.63, pred[512]{0:T(512)(128)(4,1)S(1)} %iota_compare_fusion.1), kind=kOutput, calls=%fused_computation.23 | convolution fusion | flops 540278784 | bytes 3149316 | tf_op jit(solution)/shard_map/dot_general | solution.py:77
  194.4 3.4 %fusion.18 = bf16[16,1,128,256]{3,2,0,1:T(8,128)(2,1)S(1)} fusion(bf16[16,128,512]{1,0,2:T(8,128)(2,1)S(1)} %fusion.1, f32[]{:T(128)} %bitcast.14, s32[256]{0:T(256)S(1)} %iota_add_fusion, s32[512]{0:T(512)S(1)} %fusion.63, pred[512]{0:T(512)(128)(4,1)S(1)} %iota_compare_fusion.1), kind=kOutput, calls=%fused_computation.24 | convolution fusion | flops 540278784 | bytes 3149316 | tf_op jit(solution)/shard_map/dot_general | solution.py:77
  198.1 3.4 %fusion.21 = bf16[16,1,128,256]{3,2,0,1:T(8,128)(2,1)S(1)} fusion(bf16[16,128,512]{1,0,2:T(8,128)(2,1)S(1)} %fusion.2, f32[]{:T(128)} %bitcast.20, s32[256]{0:T(256)S(1)} %iota_add_fusion, s32[512]{0:T(512)S(1)} %fusion.63, pred[512]{0:T(512)(128)(4,1)S(1)} %iota_compare_fusion.1), kind=kOutput, calls=%fused_computation.25 | convolution fusion | flops 540278784 | bytes 3149316 | tf_op jit(solution)/shard_map/dot_general | solution.py:77
  201.5 2.0 pad_maximum_fusion
  203.6 1.3 dynamic-slice.3
  205.5 93.2 %all-reduce.3.cloned.1.call-done = bf16[16,3,128,256]{3,2,0,1:T(8,128)(2,1)} async-done(((bf16[16,3,128,256]{3,2,0,1:T(8,128)(2,1)}), bf16[16,3,128,256]{3,2,0,1:T(8,128)(2,1)}) %all-reduce.3.cloned.1.call-update) | async-done | bytes 3145744
  298.7 1.3 multiply_convert_fusion.3
  300.0 0.9 copy.34
  (85 shorter events, 7.6 us)
Async XLA Ops:
  6.5 21.8 %copy-start.3 = (s32[1,3]{1,0:T(1,128)S(1)}, s32[1,3]{1,0:T(1,128)}, u32[]{:S(2)}) copy-start(s32[1,3]{1,0:T(1,128)} %param.5) | copy-start | bytes 40
  9.7 49.7 %copy-start.4 = (s32[1,16]{1,0:T(1,128)S(1)}, s32[1,16]{1,0:T(1,128)}, u32[]{:S(2)}) copy-start(s32[1,16]{1,0:T(1,128)} %param.4) | copy-start | bytes 196
  9.7 49.0 %all-to-all-start = ((bf16[1,8,2048]{1,0,2:T(2,128)(2,1)}), bf16[1,8,2048]{1,0,2:T(2,128)(2,1)S(1)}, u32[]{:S(2)}, u32[]{:S(2)}) async-start(bf16[1,8,2048]{1,0,2:T(2,128)(2,1)} %copy.19), calls=%async_computation | async-start | bytes 2097152 | tf_op jit(solution)/shard_map/all_to_all | solution.py:84
  28.2 270.5 %all-reduce.3.cloned.1.call-start = ((), (), s32[]{:S(2)}) async-start(), calls=%async_computation.1 | async-start | bytes 6291456
  62.6 19.0 %collective-permute-start = (bf16[1,16,4,512]{3,2,1,0:T(4,128)(2,1)S(1)}, bf16[1,16,4,512]{3,2,1,0:T(4,128)(2,1)S(1)}, u32[]{:S(2)}, u32[]{:S(2)}) collective-permute-start(bf16[1,16,4,512]{3,2,1,0:T(4,128)(2,1)S(1)} %reshape.97), channel_id=1, source_target_pairs={{0,60},{4,64},{8,68},{12,72},{16,76},{20,80},{24,84},{28,88},{32,9... | collective-permute-start | bytes 196616 | tf_op jit(solution)/shard_map/ppermute | solution.py:19
  67.1 18.2 %collective-permute-start.1 = (bf16[1,16,4,512]{3,2,1,0:T(4,128)(2,1)S(1)}, bf16[1,16,4,512]{3,2,1,0:T(4,128)(2,1)S(1)}, u32[]{:S(2)}, u32[]{:S(2)}) collective-permute-start(bf16[1,16,4,512]{3,2,1,0:T(4,128)(2,1)S(1)} %reshape.97), channel_id=1, source_target_pairs={{0,56},{4,60},{8,64},{12,68},{16,72},{20,76},{24,80},{28,84},{32,8... | collective-permute-start | bytes 196616 | tf_op jit(solution)/shard_map/ppermute | solution.py:19
  68.4 22.7 %collective-permute-start.2 = (bf16[1,16,4,512]{3,2,1,0:T(4,128)(2,1)S(1)}, bf16[1,16,4,512]{3,2,1,0:T(4,128)(2,1)S(1)}, u32[]{:S(2)}, u32[]{:S(2)}) collective-permute-start(bf16[1,16,4,512]{3,2,1,0:T(4,128)(2,1)S(1)} %reshape.97), channel_id=1, source_target_pairs={{0,52},{4,56},{8,60},{12,64},{16,68},{20,72},{24,76},{28,80},{32,8... | collective-permute-start | bytes 196616 | tf_op jit(solution)/shard_map/ppermute | solution.py:19
  71.7 23.0 %collective-permute-start.3 = (bf16[1,16,4,512]{3,2,1,0:T(4,128)(2,1)S(1)}, bf16[1,16,4,512]{3,2,1,0:T(4,128)(2,1)S(1)}, u32[]{:S(2)}, u32[]{:S(2)}) collective-permute-start(bf16[1,16,4,512]{3,2,1,0:T(4,128)(2,1)S(1)} %reshape.97), channel_id=1, source_target_pairs={{0,48},{4,52},{8,56},{12,60},{16,64},{20,68},{24,72},{28,76},{32,8... | collective-permute-start | bytes 196616 | tf_op jit(solution)/shard_map/ppermute | solution.py:19
  76.5 25.5 %collective-permute-start.4 = (bf16[1,16,4,512]{3,2,1,0:T(4,128)(2,1)S(1)}, bf16[1,16,4,512]{3,2,1,0:T(4,128)(2,1)S(1)}, u32[]{:S(2)}, u32[]{:S(2)}) collective-permute-start(bf16[1,16,4,512]{3,2,1,0:T(4,128)(2,1)S(1)} %reshape.97), channel_id=1, source_target_pairs={{0,44},{4,48},{8,52},{12,56},{16,60},{20,64},{24,68},{28,72},{32,7... | collective-permute-start | bytes 196616 | tf_op jit(solution)/shard_map/ppermute | solution.py:19
  81.6 21.7 %collective-permute-start.5 = (bf16[1,16,4,512]{3,2,1,0:T(4,128)(2,1)S(1)}, bf16[1,16,4,512]{3,2,1,0:T(4,128)(2,1)S(1)}, u32[]{:S(2)}, u32[]{:S(2)}) collective-permute-start(bf16[1,16,4,512]{3,2,1,0:T(4,128)(2,1)S(1)} %reshape.97), channel_id=1, source_target_pairs={{0,40},{4,44},{8,48},{12,52},{16,56},{20,60},{24,64},{28,68},{32,7... | collective-permute-start | bytes 196616 | tf_op jit(solution)/shard_map/ppermute | solution.py:19
  85.3 23.0 %collective-permute-start.6 = (bf16[1,16,4,512]{3,2,1,0:T(4,128)(2,1)S(1)}, bf16[1,16,4,512]{3,2,1,0:T(4,128)(2,1)S(1)}, u32[]{:S(2)}, u32[]{:S(2)}) collective-permute-start(bf16[1,16,4,512]{3,2,1,0:T(4,128)(2,1)S(1)} %reshape.97), channel_id=1, source_target_pairs={{0,36},{4,40},{8,44},{12,48},{16,52},{20,56},{24,60},{28,64},{32,6... | collective-permute-start | bytes 196616 | tf_op jit(solution)/shard_map/ppermute | solution.py:19
  91.1 21.3 %collective-permute-start.7 = (bf16[1,16,4,512]{3,2,1,0:T(4,128)(2,1)S(1)}, bf16[1,16,4,512]{3,2,1,0:T(4,128)(2,1)S(1)}, u32[]{:S(2)}, u32[]{:S(2)}) collective-permute-start(bf16[1,16,4,512]{3,2,1,0:T(4,128)(2,1)S(1)} %reshape.97), channel_id=1, source_target_pairs={{0,32},{4,36},{8,40},{12,44},{16,48},{20,52},{24,56},{28,60},{32,6... | collective-permute-start | bytes 196616 | tf_op jit(solution)/shard_map/ppermute | solution.py:19
  94.8 22.7 %collective-permute-start.8 = (bf16[1,16,4,512]{3,2,1,0:T(4,128)(2,1)S(1)}, bf16[1,16,4,512]{3,2,1,0:T(4,128)(2,1)S(1)}, u32[]{:S(2)}, u32[]{:S(2)}) collective-permute-start(bf16[1,16,4,512]{3,2,1,0:T(4,128)(2,1)S(1)} %reshape.97), channel_id=1, source_target_pairs={{0,28},{4,32},{8,36},{12,40},{16,44},{20,48},{24,52},{28,56},{32,6... | collective-permute-start | bytes 196616 | tf_op jit(solution)/shard_map/ppermute | solution.py:19
  102.0 17.3 %collective-permute-start.9 = (bf16[1,16,4,512]{3,2,1,0:T(4,128)(2,1)S(1)}, bf16[1,16,4,512]{3,2,1,0:T(4,128)(2,1)S(1)}, u32[]{:S(2)}, u32[]{:S(2)}) collective-permute-start(bf16[1,16,4,512]{3,2,1,0:T(4,128)(2,1)S(1)} %reshape.97), channel_id=1, source_target_pairs={{0,24},{4,28},{8,32},{12,36},{16,40},{20,44},{24,48},{28,52},{32,5... | collective-permute-start | bytes 196616 | tf_op jit(solution)/shard_map/ppermute | solution.py:19
  103.3 18.7 %collective-permute-start.10 = (bf16[1,16,4,512]{3,2,1,0:T(4,128)(2,1)S(1)}, bf16[1,16,4,512]{3,2,1,0:T(4,128)(2,1)S(1)}, u32[]{:S(2)}, u32[]{:S(2)}) collective-permute-start(bf16[1,16,4,512]{3,2,1,0:T(4,128)(2,1)S(1)} %reshape.97), channel_id=1, source_target_pairs={{0,20},{4,24},{8,28},{12,32},{16,36},{20,40},{24,44},{28,48},{32,5... | collective-permute-start | bytes 196616 | tf_op jit(solution)/shard_map/ppermute | solution.py:19
  108.3 15.6 %collective-permute-start.11 = (bf16[1,16,4,512]{3,2,1,0:T(4,128)(2,1)S(1)}, bf16[1,16,4,512]{3,2,1,0:T(4,128)(2,1)S(1)}, u32[]{:S(2)}, u32[]{:S(2)}) collective-permute-start(bf16[1,16,4,512]{3,2,1,0:T(4,128)(2,1)S(1)} %reshape.97), channel_id=1, source_target_pairs={{0,16},{4,20},{8,24},{12,28},{16,32},{20,36},{24,40},{28,44},{32,4... | collective-permute-start | bytes 196616 | tf_op jit(solution)/shard_map/ppermute | solution.py:19
  112.4 12.9 %collective-permute-start.12 = (bf16[1,16,4,512]{3,2,1,0:T(4,128)(2,1)S(1)}, bf16[1,16,4,512]{3,2,1,0:T(4,128)(2,1)S(1)}, u32[]{:S(2)}, u32[]{:S(2)}) collective-permute-start(bf16[1,16,4,512]{3,2,1,0:T(4,128)(2,1)S(1)} %reshape.97), channel_id=1, source_target_pairs={{0,12},{4,16},{8,20},{12,24},{16,28},{20,32},{24,36},{28,40},{32,4... | collective-permute-start | bytes 196616 | tf_op jit(solution)/shard_map/ppermute | solution.py:19
  117.5 9.2 %collective-permute-start.13 = (bf16[1,16,4,512]{3,2,1,0:T(4,128)(2,1)S(1)}, bf16[1,16,4,512]{3,2,1,0:T(4,128)(2,1)S(1)}, u32[]{:S(2)}, u32[]{:S(2)}) collective-permute-start(bf16[1,16,4,512]{3,2,1,0:T(4,128)(2,1)S(1)} %reshape.97), channel_id=1, source_target_pairs={{0,8},{4,12},{8,16},{12,20},{16,24},{20,28},{24,32},{28,36},{32,40... | collective-permute-start | bytes 196616 | tf_op jit(solution)/shard_map/ppermute | solution.py:19
  119.3 8.8 %collective-permute-start.14 = (bf16[1,16,4,512]{3,2,1,0:T(4,128)(2,1)S(1)}, bf16[1,16,4,512]{3,2,1,0:T(4,128)(2,1)S(1)}, u32[]{:S(2)}, u32[]{:S(2)}) collective-permute-start(bf16[1,16,4,512]{3,2,1,0:T(4,128)(2,1)S(1)} %reshape.97), channel_id=1, source_target_pairs={{0,4},{4,8},{8,12},{12,16},{16,20},{20,24},{24,28},{28,32},{32,36}... | collective-permute-start | bytes 196616 | tf_op jit(solution)/shard_map/ppermute | solution.py:19
  122.0 7.4 %collective-permute-start.15 = (bf16[1,16,4,512]{3,2,1,0:T(4,128)(2,1)S(1)}, bf16[1,16,4,512]{3,2,1,0:T(4,128)(2,1)S(1)}, u32[]{:S(2)}, u32[]{:S(2)}) collective-permute-start(bf16[1,16,4,512]{3,2,1,0:T(4,128)(2,1)S(1)} %reshape.97), channel_id=1, source_target_pairs={{4,0},{8,4},{12,8},{16,12},{20,16},{24,20},{28,24},{32,28},{36,32}... | collective-permute-start | bytes 196616 | tf_op jit(solution)/shard_map/ppermute | solution.py:19
  124.0 6.8 %collective-permute-start.16 = (bf16[1,16,4,512]{3,2,1,0:T(4,128)(2,1)S(1)}, bf16[1,16,4,512]{3,2,1,0:T(4,128)(2,1)S(1)}, u32[]{:S(2)}, u32[]{:S(2)}) collective-permute-start(bf16[1,16,4,512]{3,2,1,0:T(4,128)(2,1)S(1)} %reshape.97), channel_id=1, source_target_pairs={{8,0},{12,4},{16,8},{20,12},{24,16},{28,20},{32,24},{36,28},{40,32... | collective-permute-start | bytes 196616 | tf_op jit(solution)/shard_map/ppermute | solution.py:19
  125.3 8.3 %collective-permute-start.17 = (bf16[1,16,4,512]{3,2,1,0:T(4,128)(2,1)S(1)}, bf16[1,16,4,512]{3,2,1,0:T(4,128)(2,1)S(1)}, u32[]{:S(2)}, u32[]{:S(2)}) collective-permute-start(bf16[1,16,4,512]{3,2,1,0:T(4,128)(2,1)S(1)} %reshape.97), channel_id=1, source_target_pairs={{12,0},{16,4},{20,8},{24,12},{28,16},{32,20},{36,24},{40,28},{44,3... | collective-permute-start | bytes 196616 | tf_op jit(solution)/shard_map/ppermute | solution.py:19
  126.7 8.9 %collective-permute-start.18 = (bf16[1,16,4,512]{3,2,1,0:T(4,128)(2,1)S(1)}, bf16[1,16,4,512]{3,2,1,0:T(4,128)(2,1)S(1)}, u32[]{:S(2)}, u32[]{:S(2)}) collective-permute-start(bf16[1,16,4,512]{3,2,1,0:T(4,128)(2,1)S(1)} %reshape.97), channel_id=1, source_target_pairs={{16,0},{20,4},{24,8},{28,12},{32,16},{36,20},{40,24},{44,28},{48,3... | collective-permute-start | bytes 196616 | tf_op jit(solution)/shard_map/ppermute | solution.py:19
  128.0 11.7 %collective-permute-start.19 = (bf16[1,16,4,512]{3,2,1,0:T(4,128)(2,1)S(1)}, bf16[1,16,4,512]{3,2,1,0:T(4,128)(2,1)S(1)}, u32[]{:S(2)}, u32[]{:S(2)}) collective-permute-start(bf16[1,16,4,512]{3,2,1,0:T(4,128)(2,1)S(1)} %reshape.97), channel_id=1, source_target_pairs={{20,0},{24,4},{28,8},{32,12},{36,16},{40,20},{44,24},{48,28},{52,3... | collective-permute-start | bytes 196616 | tf_op jit(solution)/shard_map/ppermute | solution.py:19
  129.4 14.1 %collective-permute-start.20 = (bf16[1,16,4,512]{3,2,1,0:T(4,128)(2,1)S(1)}, bf16[1,16,4,512]{3,2,1,0:T(4,128)(2,1)S(1)}, u32[]{:S(2)}, u32[]{:S(2)}) collective-permute-start(bf16[1,16,4,512]{3,2,1,0:T(4,128)(2,1)S(1)} %reshape.97), channel_id=1, source_target_pairs={{24,0},{28,4},{32,8},{36,12},{40,16},{44,20},{48,24},{52,28},{56,3... | collective-permute-start | bytes 196616 | tf_op jit(solution)/shard_map/ppermute | solution.py:19
  130.8 14.1 %collective-permute-start.21 = (bf16[1,16,4,512]{3,2,1,0:T(4,128)(2,1)S(1)}, bf16[1,16,4,512]{3,2,1,0:T(4,128)(2,1)S(1)}, u32[]{:S(2)}, u32[]{:S(2)}) collective-permute-start(bf16[1,16,4,512]{3,2,1,0:T(4,128)(2,1)S(1)} %reshape.97), channel_id=1, source_target_pairs={{28,0},{32,4},{36,8},{40,12},{44,16},{48,20},{52,24},{56,28},{60,3... | collective-permute-start | bytes 196616 | tf_op jit(solution)/shard_map/ppermute | solution.py:19
  133.6 12.7 %collective-permute-start.22 = (bf16[1,16,4,512]{3,2,1,0:T(4,128)(2,1)S(1)}, bf16[1,16,4,512]{3,2,1,0:T(4,128)(2,1)S(1)}, u32[]{:S(2)}, u32[]{:S(2)}) collective-permute-start(bf16[1,16,4,512]{3,2,1,0:T(4,128)(2,1)S(1)} %reshape.97), channel_id=1, source_target_pairs={{32,0},{36,4},{40,8},{44,12},{48,16},{52,20},{56,24},{60,28},{64,3... | collective-permute-start | bytes 196616 | tf_op jit(solution)/shard_map/ppermute | solution.py:19
  135.6 13.1 %collective-permute-start.23 = (bf16[1,16,4,512]{3,2,1,0:T(4,128)(2,1)S(1)}, bf16[1,16,4,512]{3,2,1,0:T(4,128)(2,1)S(1)}, u32[]{:S(2)}, u32[]{:S(2)}) collective-permute-start(bf16[1,16,4,512]{3,2,1,0:T(4,128)(2,1)S(1)} %reshape.97), channel_id=1, source_target_pairs={{36,0},{40,4},{44,8},{48,12},{52,16},{56,20},{60,24},{64,28},{68,3... | collective-permute-start | bytes 196616 | tf_op jit(solution)/shard_map/ppermute | solution.py:19
  139.8 11.6 %collective-permute-start.24 = (bf16[1,16,4,512]{3,2,1,0:T(4,128)(2,1)S(1)}, bf16[1,16,4,512]{3,2,1,0:T(4,128)(2,1)S(1)}, u32[]{:S(2)}, u32[]{:S(2)}) collective-permute-start(bf16[1,16,4,512]{3,2,1,0:T(4,128)(2,1)S(1)} %reshape.97), channel_id=1, source_target_pairs={{40,0},{44,4},{48,8},{52,12},{56,16},{60,20},{64,24},{68,28},{72,3... | collective-permute-start | bytes 196616 | tf_op jit(solution)/shard_map/ppermute | solution.py:19
  143.5 13.5 %collective-permute-start.25 = (bf16[1,16,4,512]{3,2,1,0:T(4,128)(2,1)S(1)}, bf16[1,16,4,512]{3,2,1,0:T(4,128)(2,1)S(1)}, u32[]{:S(2)}, u32[]{:S(2)}) collective-permute-start(bf16[1,16,4,512]{3,2,1,0:T(4,128)(2,1)S(1)} %reshape.97), channel_id=1, source_target_pairs={{44,0},{48,4},{52,8},{56,12},{60,16},{64,20},{68,24},{72,28},{76,3... | collective-permute-start | bytes 196616 | tf_op jit(solution)/shard_map/ppermute | solution.py:19
  144.8 14.9 %collective-permute-start.26 = (bf16[1,16,4,512]{3,2,1,0:T(4,128)(2,1)S(1)}, bf16[1,16,4,512]{3,2,1,0:T(4,128)(2,1)S(1)}, u32[]{:S(2)}, u32[]{:S(2)}) collective-permute-start(bf16[1,16,4,512]{3,2,1,0:T(4,128)(2,1)S(1)} %reshape.97), channel_id=1, source_target_pairs={{48,0},{52,4},{56,8},{60,12},{64,16},{68,20},{72,24},{76,28},{80,3... | collective-permute-start | bytes 196616 | tf_op jit(solution)/shard_map/ppermute | solution.py:19
  146.3 21.7 %collective-permute-start.27 = (bf16[1,16,4,512]{3,2,1,0:T(4,128)(2,1)S(1)}, bf16[1,16,4,512]{3,2,1,0:T(4,128)(2,1)S(1)}, u32[]{:S(2)}, u32[]{:S(2)}) collective-permute-start(bf16[1,16,4,512]{3,2,1,0:T(4,128)(2,1)S(1)} %reshape.97), channel_id=1, source_target_pairs={{52,0},{56,4},{60,8},{64,12},{68,16},{72,20},{76,24},{80,28},{84,3... | collective-permute-start | bytes 196616 | tf_op jit(solution)/shard_map/ppermute | solution.py:19
  148.7 19.8 %collective-permute-start.28 = (bf16[1,16,4,512]{3,2,1,0:T(4,128)(2,1)S(1)}, bf16[1,16,4,512]{3,2,1,0:T(4,128)(2,1)S(1)}, u32[]{:S(2)}, u32[]{:S(2)}) collective-permute-start(bf16[1,16,4,512]{3,2,1,0:T(4,128)(2,1)S(1)} %reshape.97), channel_id=1, source_target_pairs={{56,0},{60,4},{64,8},{68,12},{72,16},{76,20},{80,24},{84,28},{88,3... | collective-permute-start | bytes 196616 | tf_op jit(solution)/shard_map/ppermute | solution.py:19
  151.4 19.3 %collective-permute-start.29 = (bf16[1,16,4,512]{3,2,1,0:T(4,128)(2,1)S(1)}, bf16[1,16,4,512]{3,2,1,0:T(4,128)(2,1)S(1)}, u32[]{:S(2)}, u32[]{:S(2)}) collective-permute-start(bf16[1,16,4,512]{3,2,1,0:T(4,128)(2,1)S(1)} %reshape.97), channel_id=1, source_target_pairs={{60,0},{64,4},{68,8},{72,12},{76,16},{80,20},{84,24},{88,28},{92,3... | collective-permute-start | bytes 196616 | tf_op jit(solution)/shard_map/ppermute | solution.py:19
  186.8 1.6 copy-start
  188.4 1.6 copy-start.1
  188.4 2.2 copy-start.2
Sparse Core Ops, SparseCore 0:
  203.7 94.9 all-reduce.2
where the time goes:
time: 309 us; the launch traced here: 308 us
  waiting for transfers between devices  147 us (48%)
  starting transfers between devices  96.5 us (31%)
  matrix products  20.7 us (7%)
  local copies, waits for them, and re-layouts  20.3 us (7%)
  between operations  18.6 us (6%)
  other arithmetic  4.67 us (2%)
    unnamed x2, waiting for transfers between devices  93.2 us
    ppermute x30, starting transfers between devices, from_behind(): lax.ppermute(value, axis, [(source, source + steps) for source in range(i...  77.9 us
    ppermute x30, waiting for transfers between devices, from_behind(): lax.ppermute(value, axis, [(source, source + steps) for source in range(i...  27.9 us
    all_to_all x1, waiting for transfers between devices, local(): lax.all_to_all(raw, 'ch', split_axis=2, concat_axis=1, tiled=True)  25.9 us
    all_to_all x1, starting transfers between devices, local(): lax.all_to_all(raw, 'ch', split_axis=2, concat_axis=1, tiled=True)  18.5 us
    dot_general x3, matrix products, correlate(): jnp.dot(cross_spec.reshape(-1, 2 * half_len), inverse, preferred_element_...  10.2 us
    unnamed x42, local copies, waits for them, and re-layouts  8.24 us
    dynamic_slice x4, local copies, waits for them, and re-layouts, local(): sources = lax.dynamic_slice_in_dim(window[0], source_start, SRC, 0)  6.39 us
  transfers between devices with their start and end apart: 32, of which 14 were waited for; matrix products, arithmetic and copies ran while one was open for 1% of the time, Pallas kernels for 0%

commit v1 on v0

--- a/solution.py
+++ b/solution.py
@@ -11,6 +11,12 @@
 MAXP = 3
 REACH = 15
 lag_scale = 1.0 / 16.0
+
+
+def trade_parts(x, axis, split, join):
+    parts = jnp.split(x, lax.axis_size(axis), axis=split)
+    received = lax.all_to_all(jnp.stack(parts), axis, 0, 0)
+    return jnp.concatenate(received, axis=join)
 
 
 def from_behind(value, axis, steps):
@@ -81,7 +87,7 @@
 
 
 def local(raw, order, pair_blocks):
-    recorded = lax.all_to_all(raw, "ch", split_axis=2, concat_axis=1, tiled=True)
+    recorded = trade_parts(raw, "ch", 2, 1)
     local_channels = recorded.shape[2]
     onehot = (order[0][:, None] == jnp.arange(local_channels, dtype=jnp.int32)[None, :]).astype(
         jnp.bfloat16

time: 309 us -> 461 us (1.49)
  local copies, waits for them, and re-layouts: 20.3 us -> 186 us
  waiting for transfers between devices: 147 us -> 130 us
    unnamed x42 -> x164, local copies, waits for them, and re-layouts: 8.24 us -> 173 us
    all_to_all x1, waiting for transfers between devices: 25.9 us -> 8.93 us  [trade_parts(): received = lax.all_to_all(jnp.stack(parts), axis, 0, 0)]
  transfers between devices with their start and end apart: 32 -> 32, of which waited for: 14 -> 12; matrix products, arithmetic and copies ran while one was open for 1% -> 1% of each run, Pallas kernels for 0% -> 0%
where the time goes in v1:
time: 461 us; the launch traced here: 457 us
  local copies, waits for them, and re-layouts  186 us (40%)
  waiting for transfers between devices  130 us (28%)
  starting transfers between devices  95.9 us (21%)
  matrix products  21.4 us (5%)
  between operations  18.6 us (4%)
  other arithmetic  4.68 us (1%)
    unnamed x164, local copies, waits for them, and re-layouts  173 us
    unnamed x2, waiting for transfers between devices  93.3 us
    ppermute x30, starting transfers between devices, from_behind(): lax.ppermute(value, axis, [(source, source + steps) for source in range(i...  77.5 us
    ppermute x30, waiting for transfers between devices, from_behind(): lax.ppermute(value, axis, [(source, source + steps) for source in range(i...  27.6 us
    all_to_all x1, starting transfers between devices, trade_parts(): received = lax.all_to_all(jnp.stack(parts), axis, 0, 0)  18.4 us
    dot_general x3, matrix products, correlate(): jnp.dot(cross_spec.reshape(-1, 2 * half_len), inverse, preferred_element_...  10.2 us
  transfers between devices with their start and end apart: 32, of which 12 were waited for; matrix products, arithmetic and copies ran while one was open for 1% of the time, Pallas kernels for 0%

profile of v1, /device:TPU:1, one launch (start us, length us, event | category | flops | bytes accessed | tf_op | source)
XLA Modules:
  0.0 456.8 jit_solution(9434692322281128259)
XLA Ops:
  7.8 1.3 constant_dynamic-update-slice_fusion.126
  9.1 1.3 constant_dynamic-update-slice_fusion.125
  10.5 1.3 constant_dynamic-update-slice_fusion.124
  11.8 1.3 constant_dynamic-update-slice_fusion.123
  13.1 1.3 constant_dynamic-update-slice_fusion.122
  14.4 1.3 constant_dynamic-update-slice_fusion.121
  15.8 1.3 constant_dynamic-update-slice_fusion.120
  18.4 1.3 constant_dynamic-update-slice_fusion.118
  19.7 1.3 constant_dynamic-update-slice_fusion.117
  21.0 1.3 constant_dynamic-update-slice_fusion.116
  22.4 1.3 constant_dynamic-update-slice_fusion.115
  23.7 1.3 constant_dynamic-update-slice_fusion.114
  25.0 1.3 constant_dynamic-update-slice_fusion.113
  26.4 1.3 constant_dynamic-update-slice_fusion.112
  28.9 1.3 constant_dynamic-update-slice_fusion.110
  30.3 1.3 constant_dynamic-update-slice_fusion.109
  31.6 1.3 constant_dynamic-update-slice_fusion.108
  32.9 1.3 constant_dynamic-update-slice_fusion.107
  34.3 1.3 constant_dynamic-update-slice_fusion.106
  35.6 1.3 constant_dynamic-update-slice_fusion.105
  36.9 1.3 constant_dynamic-update-slice_fusion.104
  39.5 1.3 constant_dynamic-update-slice_fusion.102
  40.8 1.3 constant_dynamic-update-slice_fusion.101
  42.2 1.3 constant_dynamic-update-slice_fusion.100
  43.5 1.3 constant_dynamic-update-slice_fusion.99
  175.7 18.4 %all-to-all-start = ((bf16[128,1,8,16]{3,2,1,0:T(8,128)(2,1)}), bf16[128,1,8,16]{3,2,1,0:T(8,128)(2,1)S(1)}, u32[]{:S(2)}, u32[]{:S(2)}) async-start(bf16[128,1,8,16]{3,2,1,0:T(8,128)(2,1)} %constant_dynamic-update-slice_fusion), calls=%async_computation | async-start | bytes 524288 | tf_op jit(solution)/shard_map/all_to_all | solution.py:18
  194.2 1.4 fusion.98
  199.4 8.9 %all-to-all-done = bf16[128,1,8,16]{3,2,1,0:T(8,128)(2,1)S(1)} async-done(((bf16[128,1,8,16]{3,2,1,0:T(8,128)(2,1)}), bf16[128,1,8,16]{3,2,1,0:T(8,128)(2,1)S(1)}, u32[]{:S(2)}, u32[]{:S(2)}) %all-to-all-start) | async-done | bytes 32800 | tf_op jit(solution)/shard_map/all_to_all | solution.py:18
  209.3 2.4 fusion.47
  212.2 4.0 collective-permute-start
  216.2 1.6 collective-permute-start.1
  217.9 3.2 collective-permute-start.2
  221.0 4.7 %collective-permute-start.3 = (bf16[1,16,4,512]{3,2,1,0:T(4,128)(2,1)S(1)}, bf16[1,16,4,512]{3,2,1,0:T(4,128)(2,1)S(1)}, u32[]{:S(2)}, u32[]{:S(2)}) collective-permute-start(bf16[1,16,4,512]{3,2,1,0:T(4,128)(2,1)S(1)} %reshape.96), channel_id=1, source_target_pairs={{0,48},{4,52},{8,56},{12,60},{16,64},{20,68},{24,72},{28,76},{32,8... | collective-permute-start | bytes 196616 | tf_op jit(solution)/shard_map/ppermute | solution.py:25
  225.8 4.6 collective-permute-start.4
  231.2 3.2 collective-permute-start.5
  234.4 6.0 %collective-permute-start.6 = (bf16[1,16,4,512]{3,2,1,0:T(4,128)(2,1)S(1)}, bf16[1,16,4,512]{3,2,1,0:T(4,128)(2,1)S(1)}, u32[]{:S(2)}, u32[]{:S(2)}) collective-permute-start(bf16[1,16,4,512]{3,2,1,0:T(4,128)(2,1)S(1)} %reshape.96), channel_id=1, source_target_pairs={{0,36},{4,40},{8,44},{12,48},{16,52},{20,56},{24,60},{28,64},{32,6... | collective-permute-start | bytes 196616 | tf_op jit(solution)/shard_map/ppermute | solution.py:25
  240.4 3.9 collective-permute-start.7
  244.4 6.6 %collective-permute-start.8 = (bf16[1,16,4,512]{3,2,1,0:T(4,128)(2,1)S(1)}, bf16[1,16,4,512]{3,2,1,0:T(4,128)(2,1)S(1)}, u32[]{:S(2)}, u32[]{:S(2)}) collective-permute-start(bf16[1,16,4,512]{3,2,1,0:T(4,128)(2,1)S(1)} %reshape.96), channel_id=1, source_target_pairs={{0,28},{4,32},{8,36},{12,40},{16,44},{20,48},{24,52},{28,56},{32,6... | collective-permute-start | bytes 196616 | tf_op jit(solution)/shard_map/ppermute | solution.py:25
  251.1 1.8 collective-permute-start.9
  252.9 5.4 %collective-permute-start.10 = (bf16[1,16,4,512]{3,2,1,0:T(4,128)(2,1)S(1)}, bf16[1,16,4,512]{3,2,1,0:T(4,128)(2,1)S(1)}, u32[]{:S(2)}, u32[]{:S(2)}) collective-permute-start(bf16[1,16,4,512]{3,2,1,0:T(4,128)(2,1)S(1)} %reshape.96), channel_id=1, source_target_pairs={{0,20},{4,24},{8,28},{12,32},{16,36},{20,40},{24,44},{28,48},{32,5... | collective-permute-start | bytes 196616 | tf_op jit(solution)/shard_map/ppermute | solution.py:25
  258.3 3.9 collective-permute-start.11
  262.3 4.1 collective-permute-start.12
  266.5 1.6 collective-permute-start.13
  268.1 2.8 collective-permute-start.14
  271.0 1.9 collective-permute-start.15
  281.1 1.5 collective-permute-done.17
  285.9 3.8 collective-permute-done.19
  291.0 2.7 collective-permute-done.20
  300.0 1.5 collective-permute-start.29
  301.5 5.2 %collective-permute-done.25 = bf16[1,16,4,512]{3,2,1,0:T(4,128)(2,1)S(1)} collective-permute-done((bf16[1,16,4,512]{3,2,1,0:T(4,128)(2,1)S(1)}, bf16[1,16,4,512]{3,2,1,0:T(4,128)(2,1)S(1)}, u32[]{:S(2)}, u32[]{:S(2)}) %collective-permute-start.25) | collective-permute-done | bytes 65568 | tf_op jit(solution)/shard_map/ppermute | solution.py:25
  306.8 2.3 collective-permute-done.26
  309.1 8.1 %collective-permute-done.27 = bf16[1,16,4,512]{3,2,1,0:T(4,128)(2,1)S(1)} collective-permute-done((bf16[1,16,4,512]{3,2,1,0:T(4,128)(2,1)S(1)}, bf16[1,16,4,512]{3,2,1,0:T(4,128)(2,1)S(1)}, u32[]{:S(2)}, u32[]{:S(2)}) %collective-permute-start.27) | collective-permute-done | bytes 65568 | tf_op jit(solution)/shard_map/ppermute | solution.py:25
  317.7 2.0 collective-permute-done.29
  319.7 1.5 constant_dynamic-slice_fusion.2
  322.5 2.0 convolution_bitcast_fusion.4
  324.5 2.1 copy.418
  327.9 2.0 convolution_bitcast_fusion.3
  329.8 1.9 convolution_bitcast_fusion.2
  331.8 2.2 copy.422
  339.9 3.4 fusion.15
  343.3 3.4 fusion.18
  347.1 3.4 fusion.21
  350.5 2.0 pad_maximum_fusion
  354.5 93.3 %all-reduce.3.cloned.1.call-done = bf16[16,3,128,256]{3,2,0,1:T(8,128)(2,1)} async-done(((bf16[16,3,128,256]{3,2,0,1:T(8,128)(2,1)}), bf16[16,3,128,256]{3,2,0,1:T(8,128)(2,1)}) %all-reduce.3.cloned.1.call-update) | async-done | bytes 3145744
  (206 shorter events, 170.5 us)
Async XLA Ops:
  175.7 32.6 %all-to-all-start = ((bf16[128,1,8,16]{3,2,1,0:T(8,128)(2,1)}), bf16[128,1,8,16]{3,2,1,0:T(8,128)(2,1)S(1)}, u32[]{:S(2)}, u32[]{:S(2)}) async-start(bf16[128,1,8,16]{3,2,1,0:T(8,128)(2,1)} %constant_dynamic-update-slice_fusion), calls=%async_computation | async-start | bytes 524288 | tf_op jit(solution)/shard_map/all_to_all | solution.py:18
  194.1 253.6 %all-reduce.3.cloned.1.call-start = ((), (), s32[]{:S(2)}) async-start(), calls=%async_computation.1 | async-start | bytes 6291456
  212.2 19.0 %collective-permute-start = (bf16[1,16,4,512]{3,2,1,0:T(4,128)(2,1)S(1)}, bf16[1,16,4,512]{3,2,1,0:T(4,128)(2,1)S(1)}, u32[]{:S(2)}, u32[]{:S(2)}) collective-permute-start(bf16[1,16,4,512]{3,2,1,0:T(4,128)(2,1)S(1)} %reshape.96), channel_id=1, source_target_pairs={{0,60},{4,64},{8,68},{12,72},{16,76},{20,80},{24,84},{28,88},{32,9... | collective-permute-start | bytes 196616 | tf_op jit(solution)/shard_map/ppermute | solution.py:25
  216.2 18.2 %collective-permute-start.1 = (bf16[1,16,4,512]{3,2,1,0:T(4,128)(2,1)S(1)}, bf16[1,16,4,512]{3,2,1,0:T(4,128)(2,1)S(1)}, u32[]{:S(2)}, u32[]{:S(2)}) collective-permute-start(bf16[1,16,4,512]{3,2,1,0:T(4,128)(2,1)S(1)} %reshape.96), channel_id=1, source_target_pairs={{0,56},{4,60},{8,64},{12,68},{16,72},{20,76},{24,80},{28,84},{32,8... | collective-permute-start | bytes 196616 | tf_op jit(solution)/shard_map/ppermute | solution.py:25
  217.9 22.6 %collective-permute-start.2 = (bf16[1,16,4,512]{3,2,1,0:T(4,128)(2,1)S(1)}, bf16[1,16,4,512]{3,2,1,0:T(4,128)(2,1)S(1)}, u32[]{:S(2)}, u32[]{:S(2)}) collective-permute-start(bf16[1,16,4,512]{3,2,1,0:T(4,128)(2,1)S(1)} %reshape.96), channel_id=1, source_target_pairs={{0,52},{4,56},{8,60},{12,64},{16,68},{20,72},{24,76},{28,80},{32,8... | collective-permute-start | bytes 196616 | tf_op jit(solution)/shard_map/ppermute | solution.py:25
  221.0 23.3 %collective-permute-start.3 = (bf16[1,16,4,512]{3,2,1,0:T(4,128)(2,1)S(1)}, bf16[1,16,4,512]{3,2,1,0:T(4,128)(2,1)S(1)}, u32[]{:S(2)}, u32[]{:S(2)}) collective-permute-start(bf16[1,16,4,512]{3,2,1,0:T(4,128)(2,1)S(1)} %reshape.96), channel_id=1, source_target_pairs={{0,48},{4,52},{8,56},{12,60},{16,64},{20,68},{24,72},{28,76},{32,8... | collective-permute-start | bytes 196616 | tf_op jit(solution)/shard_map/ppermute | solution.py:25
  225.8 25.3 %collective-permute-start.4 = (bf16[1,16,4,512]{3,2,1,0:T(4,128)(2,1)S(1)}, bf16[1,16,4,512]{3,2,1,0:T(4,128)(2,1)S(1)}, u32[]{:S(2)}, u32[]{:S(2)}) collective-permute-start(bf16[1,16,4,512]{3,2,1,0:T(4,128)(2,1)S(1)} %reshape.96), channel_id=1, source_target_pairs={{0,44},{4,48},{8,52},{12,56},{16,60},{20,64},{24,68},{28,72},{32,7... | collective-permute-start | bytes 196616 | tf_op jit(solution)/shard_map/ppermute | solution.py:25
  231.2 21.7 %collective-permute-start.5 = (bf16[1,16,4,512]{3,2,1,0:T(4,128)(2,1)S(1)}, bf16[1,16,4,512]{3,2,1,0:T(4,128)(2,1)S(1)}, u32[]{:S(2)}, u32[]{:S(2)}) collective-permute-start(bf16[1,16,4,512]{3,2,1,0:T(4,128)(2,1)S(1)} %reshape.96), channel_id=1, source_target_pairs={{0,40},{4,44},{8,48},{12,52},{16,56},{20,60},{24,64},{28,68},{32,7... | collective-permute-start | bytes 196616 | tf_op jit(solution)/shard_map/ppermute | solution.py:25
  234.4 23.9 %collective-permute-start.6 = (bf16[1,16,4,512]{3,2,1,0:T(4,128)(2,1)S(1)}, bf16[1,16,4,512]{3,2,1,0:T(4,128)(2,1)S(1)}, u32[]{:S(2)}, u32[]{:S(2)}) collective-permute-start(bf16[1,16,4,512]{3,2,1,0:T(4,128)(2,1)S(1)} %reshape.96), channel_id=1, source_target_pairs={{0,36},{4,40},{8,44},{12,48},{16,52},{20,56},{24,60},{28,64},{32,6... | collective-permute-start | bytes 196616 | tf_op jit(solution)/shard_map/ppermute | solution.py:25
  240.4 21.8 %collective-permute-start.7 = (bf16[1,16,4,512]{3,2,1,0:T(4,128)(2,1)S(1)}, bf16[1,16,4,512]{3,2,1,0:T(4,128)(2,1)S(1)}, u32[]{:S(2)}, u32[]{:S(2)}) collective-permute-start(bf16[1,16,4,512]{3,2,1,0:T(4,128)(2,1)S(1)} %reshape.96), channel_id=1, source_target_pairs={{0,32},{4,36},{8,40},{12,44},{16,48},{20,52},{24,56},{28,60},{32,6... | collective-permute-start | bytes 196616 | tf_op jit(solution)/shard_map/ppermute | solution.py:25
  244.4 22.1 %collective-permute-start.8 = (bf16[1,16,4,512]{3,2,1,0:T(4,128)(2,1)S(1)}, bf16[1,16,4,512]{3,2,1,0:T(4,128)(2,1)S(1)}, u32[]{:S(2)}, u32[]{:S(2)}) collective-permute-start(bf16[1,16,4,512]{3,2,1,0:T(4,128)(2,1)S(1)} %reshape.96), channel_id=1, source_target_pairs={{0,28},{4,32},{8,36},{12,40},{16,44},{20,48},{24,52},{28,56},{32,6... | collective-permute-start | bytes 196616 | tf_op jit(solution)/shard_map/ppermute | solution.py:25
  251.1 17.1 %collective-permute-start.9 = (bf16[1,16,4,512]{3,2,1,0:T(4,128)(2,1)S(1)}, bf16[1,16,4,512]{3,2,1,0:T(4,128)(2,1)S(1)}, u32[]{:S(2)}, u32[]{:S(2)}) collective-permute-start(bf16[1,16,4,512]{3,2,1,0:T(4,128)(2,1)S(1)} %reshape.96), channel_id=1, source_target_pairs={{0,24},{4,28},{8,32},{12,36},{16,40},{20,44},{24,48},{28,52},{32,5... | collective-permute-start | bytes 196616 | tf_op jit(solution)/shard_map/ppermute | solution.py:25
  252.9 18.1 %collective-permute-start.10 = (bf16[1,16,4,512]{3,2,1,0:T(4,128)(2,1)S(1)}, bf16[1,16,4,512]{3,2,1,0:T(4,128)(2,1)S(1)}, u32[]{:S(2)}, u32[]{:S(2)}) collective-permute-start(bf16[1,16,4,512]{3,2,1,0:T(4,128)(2,1)S(1)} %reshape.96), channel_id=1, source_target_pairs={{0,20},{4,24},{8,28},{12,32},{16,36},{20,40},{24,44},{28,48},{32,5... | collective-permute-start | bytes 196616 | tf_op jit(solution)/shard_map/ppermute | solution.py:25
  258.3 14.6 %collective-permute-start.11 = (bf16[1,16,4,512]{3,2,1,0:T(4,128)(2,1)S(1)}, bf16[1,16,4,512]{3,2,1,0:T(4,128)(2,1)S(1)}, u32[]{:S(2)}, u32[]{:S(2)}) collective-permute-start(bf16[1,16,4,512]{3,2,1,0:T(4,128)(2,1)S(1)} %reshape.96), channel_id=1, source_target_pairs={{0,16},{4,20},{8,24},{12,28},{16,32},{20,36},{24,40},{28,44},{32,4... | collective-permute-start | bytes 196616 | tf_op jit(solution)/shard_map/ppermute | solution.py:25
  262.3 12.0 %collective-permute-start.12 = (bf16[1,16,4,512]{3,2,1,0:T(4,128)(2,1)S(1)}, bf16[1,16,4,512]{3,2,1,0:T(4,128)(2,1)S(1)}, u32[]{:S(2)}, u32[]{:S(2)}) collective-permute-start(bf16[1,16,4,512]{3,2,1,0:T(4,128)(2,1)S(1)} %reshape.96), channel_id=1, source_target_pairs={{0,12},{4,16},{8,20},{12,24},{16,28},{20,32},{24,36},{28,40},{32,4... | collective-permute-start | bytes 196616 | tf_op jit(solution)/shard_map/ppermute | solution.py:25
  266.5 9.2 %collective-permute-start.13 = (bf16[1,16,4,512]{3,2,1,0:T(4,128)(2,1)S(1)}, bf16[1,16,4,512]{3,2,1,0:T(4,128)(2,1)S(1)}, u32[]{:S(2)}, u32[]{:S(2)}) collective-permute-start(bf16[1,16,4,512]{3,2,1,0:T(4,128)(2,1)S(1)} %reshape.96), channel_id=1, source_target_pairs={{0,8},{4,12},{8,16},{12,20},{16,24},{20,28},{24,32},{28,36},{32,40... | collective-permute-start | bytes 196616 | tf_op jit(solution)/shard_map/ppermute | solution.py:25
  268.1 8.8 %collective-permute-start.14 = (bf16[1,16,4,512]{3,2,1,0:T(4,128)(2,1)S(1)}, bf16[1,16,4,512]{3,2,1,0:T(4,128)(2,1)S(1)}, u32[]{:S(2)}, u32[]{:S(2)}) collective-permute-start(bf16[1,16,4,512]{3,2,1,0:T(4,128)(2,1)S(1)} %reshape.96), channel_id=1, source_target_pairs={{0,4},{4,8},{8,12},{12,16},{16,20},{20,24},{24,28},{28,32},{32,36}... | collective-permute-start | bytes 196616 | tf_op jit(solution)/shard_map/ppermute | solution.py:25
  271.0 7.4 %collective-permute-start.15 = (bf16[1,16,4,512]{3,2,1,0:T(4,128)(2,1)S(1)}, bf16[1,16,4,512]{3,2,1,0:T(4,128)(2,1)S(1)}, u32[]{:S(2)}, u32[]{:S(2)}) collective-permute-start(bf16[1,16,4,512]{3,2,1,0:T(4,128)(2,1)S(1)} %reshape.96), channel_id=1, source_target_pairs={{4,0},{8,4},{12,8},{16,12},{20,16},{24,20},{28,24},{32,28},{36,32}... | collective-permute-start | bytes 196616 | tf_op jit(solution)/shard_map/ppermute | solution.py:25
  272.9 6.8 %collective-permute-start.16 = (bf16[1,16,4,512]{3,2,1,0:T(4,128)(2,1)S(1)}, bf16[1,16,4,512]{3,2,1,0:T(4,128)(2,1)S(1)}, u32[]{:S(2)}, u32[]{:S(2)}) collective-permute-start(bf16[1,16,4,512]{3,2,1,0:T(4,128)(2,1)S(1)} %reshape.96), channel_id=1, source_target_pairs={{8,0},{12,4},{16,8},{20,12},{24,16},{28,20},{32,24},{36,28},{40,32... | collective-permute-start | bytes 196616 | tf_op jit(solution)/shard_map/ppermute | solution.py:25
  274.3 8.3 %collective-permute-start.17 = (bf16[1,16,4,512]{3,2,1,0:T(4,128)(2,1)S(1)}, bf16[1,16,4,512]{3,2,1,0:T(4,128)(2,1)S(1)}, u32[]{:S(2)}, u32[]{:S(2)}) collective-permute-start(bf16[1,16,4,512]{3,2,1,0:T(4,128)(2,1)S(1)} %reshape.96), channel_id=1, source_target_pairs={{12,0},{16,4},{20,8},{24,12},{28,16},{32,20},{36,24},{40,28},{44,3... | collective-permute-start | bytes 196616 | tf_op jit(solution)/shard_map/ppermute | solution.py:25
  275.6 8.9 %collective-permute-start.18 = (bf16[1,16,4,512]{3,2,1,0:T(4,128)(2,1)S(1)}, bf16[1,16,4,512]{3,2,1,0:T(4,128)(2,1)S(1)}, u32[]{:S(2)}, u32[]{:S(2)}) collective-permute-start(bf16[1,16,4,512]{3,2,1,0:T(4,128)(2,1)S(1)} %reshape.96), channel_id=1, source_target_pairs={{16,0},{20,4},{24,8},{28,12},{32,16},{36,20},{40,24},{44,28},{48,3... | collective-permute-start | bytes 196616 | tf_op jit(solution)/shard_map/ppermute | solution.py:25
  277.0 12.7 %collective-permute-start.19 = (bf16[1,16,4,512]{3,2,1,0:T(4,128)(2,1)S(1)}, bf16[1,16,4,512]{3,2,1,0:T(4,128)(2,1)S(1)}, u32[]{:S(2)}, u32[]{:S(2)}) collective-permute-start(bf16[1,16,4,512]{3,2,1,0:T(4,128)(2,1)S(1)} %reshape.96), channel_id=1, source_target_pairs={{20,0},{24,4},{28,8},{32,12},{36,16},{40,20},{44,24},{48,28},{52,3... | collective-permute-start | bytes 196616 | tf_op jit(solution)/shard_map/ppermute | solution.py:25
  278.4 15.3 %collective-permute-start.20 = (bf16[1,16,4,512]{3,2,1,0:T(4,128)(2,1)S(1)}, bf16[1,16,4,512]{3,2,1,0:T(4,128)(2,1)S(1)}, u32[]{:S(2)}, u32[]{:S(2)}) collective-permute-start(bf16[1,16,4,512]{3,2,1,0:T(4,128)(2,1)S(1)} %reshape.96), channel_id=1, source_target_pairs={{24,0},{28,4},{32,8},{36,12},{40,16},{44,20},{48,24},{52,28},{56,3... | collective-permute-start | bytes 196616 | tf_op jit(solution)/shard_map/ppermute | solution.py:25
  279.7 15.2 %collective-permute-start.21 = (bf16[1,16,4,512]{3,2,1,0:T(4,128)(2,1)S(1)}, bf16[1,16,4,512]{3,2,1,0:T(4,128)(2,1)S(1)}, u32[]{:S(2)}, u32[]{:S(2)}) collective-permute-start(bf16[1,16,4,512]{3,2,1,0:T(4,128)(2,1)S(1)} %reshape.96), channel_id=1, source_target_pairs={{28,0},{32,4},{36,8},{40,12},{44,16},{48,20},{52,24},{56,28},{60,3... | collective-permute-start | bytes 196616 | tf_op jit(solution)/shard_map/ppermute | solution.py:25
  282.5 13.8 %collective-permute-start.22 = (bf16[1,16,4,512]{3,2,1,0:T(4,128)(2,1)S(1)}, bf16[1,16,4,512]{3,2,1,0:T(4,128)(2,1)S(1)}, u32[]{:S(2)}, u32[]{:S(2)}) collective-permute-start(bf16[1,16,4,512]{3,2,1,0:T(4,128)(2,1)S(1)} %reshape.96), channel_id=1, source_target_pairs={{32,0},{36,4},{40,8},{44,12},{48,16},{52,20},{56,24},{60,28},{64,3... | collective-permute-start | bytes 196616 | tf_op jit(solution)/shard_map/ppermute | solution.py:25
  284.6 13.1 %collective-permute-start.23 = (bf16[1,16,4,512]{3,2,1,0:T(4,128)(2,1)S(1)}, bf16[1,16,4,512]{3,2,1,0:T(4,128)(2,1)S(1)}, u32[]{:S(2)}, u32[]{:S(2)}) collective-permute-start(bf16[1,16,4,512]{3,2,1,0:T(4,128)(2,1)S(1)} %reshape.96), channel_id=1, source_target_pairs={{36,0},{40,4},{44,8},{48,12},{52,16},{56,20},{60,24},{64,28},{68,3... | collective-permute-start | bytes 196616 | tf_op jit(solution)/shard_map/ppermute | solution.py:25
  289.6 10.4 %collective-permute-start.24 = (bf16[1,16,4,512]{3,2,1,0:T(4,128)(2,1)S(1)}, bf16[1,16,4,512]{3,2,1,0:T(4,128)(2,1)S(1)}, u32[]{:S(2)}, u32[]{:S(2)}) collective-permute-start(bf16[1,16,4,512]{3,2,1,0:T(4,128)(2,1)S(1)} %reshape.96), channel_id=1, source_target_pairs={{40,0},{44,4},{48,8},{52,12},{56,16},{60,20},{64,24},{68,28},{72,3... | collective-permute-start | bytes 196616 | tf_op jit(solution)/shard_map/ppermute | solution.py:25
  293.6 13.1 %collective-permute-start.25 = (bf16[1,16,4,512]{3,2,1,0:T(4,128)(2,1)S(1)}, bf16[1,16,4,512]{3,2,1,0:T(4,128)(2,1)S(1)}, u32[]{:S(2)}, u32[]{:S(2)}) collective-permute-start(bf16[1,16,4,512]{3,2,1,0:T(4,128)(2,1)S(1)} %reshape.96), channel_id=1, source_target_pairs={{44,0},{48,4},{52,8},{56,12},{60,16},{64,20},{68,24},{72,28},{76,3... | collective-permute-start | bytes 196616 | tf_op jit(solution)/shard_map/ppermute | solution.py:25
  295.0 14.1 %collective-permute-start.26 = (bf16[1,16,4,512]{3,2,1,0:T(4,128)(2,1)S(1)}, bf16[1,16,4,512]{3,2,1,0:T(4,128)(2,1)S(1)}, u32[]{:S(2)}, u32[]{:S(2)}) collective-permute-start(bf16[1,16,4,512]{3,2,1,0:T(4,128)(2,1)S(1)} %reshape.96), channel_id=1, source_target_pairs={{48,0},{52,4},{56,8},{60,12},{64,16},{68,20},{72,24},{76,28},{80,3... | collective-permute-start | bytes 196616 | tf_op jit(solution)/shard_map/ppermute | solution.py:25
  296.3 20.8 %collective-permute-start.27 = (bf16[1,16,4,512]{3,2,1,0:T(4,128)(2,1)S(1)}, bf16[1,16,4,512]{3,2,1,0:T(4,128)(2,1)S(1)}, u32[]{:S(2)}, u32[]{:S(2)}) collective-permute-start(bf16[1,16,4,512]{3,2,1,0:T(4,128)(2,1)S(1)} %reshape.96), channel_id=1, source_target_pairs={{52,0},{56,4},{60,8},{64,12},{68,16},{72,20},{76,24},{80,28},{84,3... | collective-permute-start | bytes 196616 | tf_op jit(solution)/shard_map/ppermute | solution.py:25
  297.7 20.0 %collective-permute-start.28 = (bf16[1,16,4,512]{3,2,1,0:T(4,128)(2,1)S(1)}, bf16[1,16,4,512]{3,2,1,0:T(4,128)(2,1)S(1)}, u32[]{:S(2)}, u32[]{:S(2)}) collective-permute-start(bf16[1,16,4,512]{3,2,1,0:T(4,128)(2,1)S(1)} %reshape.96), channel_id=1, source_target_pairs={{56,0},{60,4},{64,8},{68,12},{72,16},{76,20},{80,24},{84,28},{88,3... | collective-permute-start | bytes 196616 | tf_op jit(solution)/shard_map/ppermute | solution.py:25
  300.0 19.6 %collective-permute-start.29 = (bf16[1,16,4,512]{3,2,1,0:T(4,128)(2,1)S(1)}, bf16[1,16,4,512]{3,2,1,0:T(4,128)(2,1)S(1)}, u32[]{:S(2)}, u32[]{:S(2)}) collective-permute-start(bf16[1,16,4,512]{3,2,1,0:T(4,128)(2,1)S(1)} %reshape.96), channel_id=1, source_target_pairs={{60,0},{64,4},{68,8},{72,12},{76,16},{80,20},{84,24},{88,28},{92,3... | collective-permute-start | bytes 196616 | tf_op jit(solution)/shard_map/ppermute | solution.py:25
  335.7 1.6 copy-start
  337.3 1.6 copy-start.1
  337.3 2.2 copy-start.2
Sparse Core Ops, SparseCore 0:
  352.6 95.0 all-reduce.2
